TPU v7x, 512 devices: a whole 4x8x8 slice. The times are simulated.
512 devices in a mesh: row: 16 (over z, core), col: 32 (over y, x).
Axes of the slice: x: 4, y: 8, z: 8, core: 2. Of those that a mesh axis runs over, the one named last changes fastest.
Arguments:
- initial_voltage: float32 [16, 64, 128, 128], P('row', 'col'), may hold values from -6 to 6
- inject: float32 [16, 64, 128, 128], P('row', 'col'), may hold values from -6 to 6
- conduct: float32 [16, 64, 128, 128], P('row', 'col'), as said below
- capacitance: float32 [16, 64, 128], P('row', 'col'), may hold values from 1 to 4
- track_gain: float32 [16, 64, 2, 32], P('row', 'col'), may hold values from 0.3 to 3
- driver_tile: int32 [16, 32, 64], P('row', 'col'), may hold values from 0 to 1
- sink_net: int32 [16, 32, 32, 8], P('row', 'col'), may hold values from 0 to 63
- sink_count: int32 [16, 32, 32], P('row', 'col'), may hold values from 0 to 8, as said below
- sink_tile: int32 [16, 32, 32, 8], P('row', 'col'), may hold values from 0 to 1
- sink_node: int32 [16, 32, 32, 8], P('row', 'col'), may hold values from 0 to 127
- sink_gain: float32 [16, 32, 32, 8], P('row', 'col'), may hold values from 0.5 to 2
Outputs:
- voltage: float32 [16, 64, 128, 128], P('row', 'col')
Inputs may be any that keep to these rules, and one draw needn't show every extreme that they name: Slots k >= sink_count[d, s] are ignored; some receiving device takes all 8 slots from some source device in every draw. `conduct`: each tile's block is symmetric with non-positive entries off the diagonal and rows summing to zero.
All inputs are finite; a program needn't handle non-finite values.
Results may differ from a plain program's by a relative error of at most 0.0001.
Values sent between devices are 32-bit elements; how exact they have to be, the bound alone decides.
A program may use at most 64 MiB of HBM per device.

v0:
```python
import jax
import jax.numpy as jnp
from jax import lax
from jax.sharding import PartitionSpec as P

ITERS = 3
PRECISE = lax.Precision.HIGHEST


def padded_2(block, sides, width):
    for axis, dim in sides:
        count = lax.axis_size(axis)
        forward = [(i, i + 1) for i in range(count - 1)]
        backward = [(target, source) for source, target in forward]
        low = lax.ppermute(
            lax.slice_in_dim(block, block.shape[dim] - width, None, axis=dim), axis, forward
        )
        high = lax.ppermute(lax.slice_in_dim(block, 0, width, axis=dim), axis, backward)
        block = jnp.concatenate([low, block, high], axis=dim)
    return block


def shifted(block, axis, distance):
    devices = range(lax.axis_size(axis))
    route = [(i - distance, i) for i in devices if i - distance in devices]
    return lax.ppermute(block, axis, route)


def tile_inverse(conduct, capacitance):
    node_count = conduct.shape[-1]
    identity = jnp.eye(node_count, dtype=jnp.float32)
    whole_block = conduct + capacitance[..., None] * identity
    flat_blocks = whole_block.reshape((-1, node_count, node_count))
    factors = jnp.linalg.cholesky(flat_blocks)
    inverse = jax.vmap(lambda factor: jax.scipy.linalg.cho_solve((factor, True), identity))(factors)
    return inverse.reshape(whole_block.shape)


def apply_grid(voltage, conduct, capacitance, track_pad):
    edge_count = track_pad.shape[-1]
    inner_part = (
        jnp.einsum("rcij,rcjp->rcip", conduct, voltage, precision=PRECISE)
        + capacitance[..., None] * voltage
    )
    rim_cells = voltage[:, :, :edge_count, :]
    padded = padded_2(rim_cells, (("row", 0), ("col", 1)), 1)
    east_gain = track_pad[1:-1, 1:-1, 0][..., None]
    west_gain = track_pad[1:-1, :-2, 0][..., None]
    south_gain = track_pad[1:-1, 1:-1, 1][..., None]
    north_gain = track_pad[:-2, 1:-1, 1][..., None]
    track_flow = east_gain * (rim_cells - padded[1:-1, 2:]) + west_gain * (
        rim_cells - padded[1:-1, :-2]
    )
    track_flow = (
        track_flow
        + south_gain * (rim_cells - padded[2:, 1:-1])
        + north_gain * (rim_cells - padded[:-2, 1:-1])
    )
    return jnp.concatenate(
        [inner_part[:, :, :edge_count] + track_flow, inner_part[:, :, edge_count:]], axis=2
    )


def precondition(inverse, residual):
    return jnp.einsum("rcij,rcjp->rcip", inverse, residual, precision=PRECISE)


def inner_sum(left_vec, right_vec):
    return jnp.sum(left_vec * right_vec, axis=(0, 1, 2))


def residual_product(residual, precond):
    return lax.psum(inner_sum(residual, precond), ("row", "col"))


def solve_separate(right_side, initial, conduct, capacitance, track_pad, inverse):
    solution = initial
    residual = right_side - apply_grid(initial, conduct, capacitance, track_pad)
    precond = precondition(inverse, residual)
    direction = precond
    rz_now = residual_product(residual, precond)
    for sweep_idx in range(ITERS):
        applied = apply_grid(direction, conduct, capacitance, track_pad)
        curvature = lax.psum(inner_sum(direction, applied), ("row", "col"))
        step_size = rz_now / curvature
        solution = solution + step_size * direction
        residual = residual - step_size * applied
        precond = precondition(inverse, residual)
        rz_fresh = residual_product(residual, precond)
        direction = precond + rz_fresh / rz_now * direction
        rz_now = rz_fresh
    return solution


def driver_voltage(voltage, driver_tile):
    node_count = voltage.shape[2]
    flat_field = voltage.reshape((-1, voltage.shape[3]))
    net_count = driver_tile.shape[-1]
    row_index = (
        driver_tile.reshape(-1) * node_count + jnp.arange(net_count, dtype=jnp.int32) % node_count
    )
    return jnp.take(flat_field, row_index, axis=0)


def sink_current(values, sink_tile, sink_node, sink_gain, sink_count, node_count, tile_count):
    source_count, slot_count, pattern_count = values.shape
    live_slot = jnp.arange(slot_count, dtype=jnp.int32)[None, :] < sink_count.reshape(
        (source_count, 1)
    )
    weight = jnp.where(live_slot, sink_gain.reshape((source_count, slot_count)), jnp.float32(0.0))
    row_index = (sink_tile * node_count + sink_node).reshape(-1)
    scaled = (values * weight[..., None]).reshape((-1, pattern_count))
    injected = jnp.zeros((tile_count * node_count, pattern_count), jnp.float32)
    return injected.at[row_index].add(scaled)


def lower_rims(track_gain):
    west_piece = shifted(track_gain[:, -1:, 0, :], "col", 1)
    north_piece = shifted(track_gain[-1:, :, 1, :], "row", 1)
    track_pad = jnp.pad(track_gain, ((1, 1), (1, 1), (0, 0), (0, 0)))
    track_pad = track_pad.at[1:-1, 0, 0].set(west_piece[:, 0])
    return track_pad.at[0, 1:-1, 1].set(north_piece[0])


def local(
    initial_voltage,
    inject,
    conduct,
    capacitance,
    track_gain,
    driver_tile,
    sink_net,
    sink_count,
    sink_tile,
    sink_node,
    sink_gain,
):
    inverse = tile_inverse(conduct, capacitance)
    track_pad = lower_rims(track_gain)
    col_count = lax.axis_size("col")
    net_count = driver_tile.shape[-1]
    pattern_count = initial_voltage.shape[3]
    node_count = initial_voltage.shape[2]
    tile_count = initial_voltage.shape[0] * initial_voltage.shape[1]
    wanted = sink_net.reshape((sink_net.shape[2], sink_net.shape[3]))
    voltage = initial_voltage
    drivers = driver_voltage(voltage, driver_tile)
    gathered = lax.all_gather(drivers, "col", axis=0, tiled=True)
    offsets = jnp.arange(col_count, dtype=jnp.int32)[:, None] * net_count
    values = jnp.take(gathered, (wanted + offsets).reshape(-1), axis=0).reshape(
        wanted.shape + (pattern_count,)
    )
    injected = sink_current(
        values, sink_tile, sink_node, sink_gain, sink_count, node_count, tile_count
    )
    right_side = capacitance[..., None] * voltage + inject + injected.reshape(voltage.shape)
    voltage = solve_separate(right_side, voltage, conduct, capacitance, track_pad, inverse)
    return voltage


def solution(mesh):
    placed = (
        P("row", "col", None, None),
        P("row", "col", None, None),
        P("row", "col", None, None),
        P("row", "col", None),
        P("row", "col", None, None),
        P("row", "col", None),
        P("row", "col", None, None),
        P("row", "col", None),
        P("row", "col", None, None),
        P("row", "col", None, None),
        P("row", "col", None, None),
    )
    return jax.shard_map(
        local, mesh=mesh, in_specs=placed, out_specs=P("row", "col", None, None), check_vma=False
    )
```

profile of v0, /device:TPU:1, one launch (start us, length us, event | category | flops | bytes accessed | tf_op | source)
XLA Modules:
  0.0 707.5 jit_solution(17942465035946714458)
XLA Ops:
  6.5 1.1 copy.150
  7.6 8.8 %collective-permute-start.2 = (f32[1,2,32,128]{2,3,1,0:T(8,128)S(1)}, f32[1,2,32,128]{2,3,1,0:T(8,128)S(1)}, u32[]{:S(2)}, u32[]{:S(2)}) collective-permute-start(f32[1,2,32,128]{2,3,1,0:T(8,128)S(1)} %bitcast.150), channel_id=1, source_target_pairs={{32,0},{64,32},{96,64},{128,96},{160,128},{192,160},{224,192},{256... | collective-permute-start | bytes 98312 | tf_op jit(solution)/shard_map/ppermute | solution.py:18
  16.4 1.9 collective-permute-start.1
  18.4 1.3 collective-permute-start
  19.7 1.9 collective-permute-start.5
  21.7 0.6 gather_fusion
  22.3 0.7 broadcast_select_fusion
  23.3 0.6 copy-done.5
  24.2 0.6 copy-done.9
  25.0 0.5 copy-done.6
  25.7 0.6 copy-done.8
  26.5 0.7 copy-done.3
  28.0 0.8 copy-done.2
  29.1 1.3 collective-permute-start.3
  30.4 4.0 collective-permute-start.4
  34.5 1.1 collective-permute-done.4
  35.9 66.4 %all-gather.2.cloned.1.call-done = f32[2048,128]{1,0:T(8,128)} async-done(((f32[64,128]{1,0:T(8,128)}), f32[2048,128]{1,0:T(8,128)}) %all-gather.2.cloned.1.call-update) | async-done | bytes 1048592 | tf_op jit(solution)/shard_map/all_gather | solution.py:148
  102.3 3.4 scatter_custom_fusion
  106.0 23.5 %custom-call.11 = f32[2,128,128]{2,1,0:T(8,128)S(1)} custom-call(f32[2,128,128]{2,1,0:T(8,128)S(1)} %fusion.13), custom_call_target="Cholesky" | custom-call | tf_op jit(solution)/shard_map/jit(cholesky)/cholesky | solution.py:34
  129.8 19.7 %custom-call.12 = f32[2,1,128,128]{2,3,1,0:T(8,128)S(1)} custom-call(f32[2,1,128,128]{3,2,1,0:T(8,128)S(1)} %select_bitcast_fusion), custom_call_target="InvertDiagBlocksLowerTriangular" | custom-call | tf_op jit(solution)/shard_map/vmap(jit(_cho_solve))/triangular_solve | solution.py:35
  151.0 6.9 collective-permute-start.7
  157.9 3.2 collective-permute-start.6
  161.3 0.5 collective-permute-done.7
  161.9 1.2 collective-permute-done.6
  163.1 1.3 collective-permute-start.8
  164.4 4.0 collective-permute-start.9
  168.6 1.0 collective-permute-done.9
  170.1 103.8 %all-reduce.1 = (f32[128]{0:T(128)S(1)}, f32[128]{0:T(128)S(1)}) all-reduce(f32[128]{0:T(128)S(1)} %multiply_reduce_fusion, f32[128]{0:T(128)S(1)} %fusion.8), channel_id=1, replica_groups=mesh['row'=16,'col'=32] {'row','col'}, use_global_device_ids=true, to_apply=%region_4.5 | all-reduce | flops 256 | bytes 2048 | tf_op jit(solution)/shard_map/psum | solution.py:73
  274.0 0.5 fusion.17
  274.5 95.4 %psum.44 = f32[128]{0:T(128)S(1)} all-reduce(f32[128]{0:T(128)S(1)} %get-tuple-element.56), channel_id=1, replica_groups=mesh['row'=16,'col'=32] {'row','col'}, use_global_device_ids=true, to_apply=%region_8.9 | all-reduce | flops 128 | bytes 1024 | tf_op jit(solution)/shard_map/psum | solution.py:73
  370.0 2.6 collective-permute-start.11
  372.6 3.3 collective-permute-start.10
  375.9 0.4 fusion.3
  376.7 1.2 collective-permute-done.10
  377.9 1.3 collective-permute-start.12
  379.2 4.0 collective-permute-start.13
  383.3 1.0 collective-permute-done.13
  384.8 102.0 %psum.45 = f32[128]{0:T(128)S(1)} all-reduce(f32[128]{0:T(128)S(1)} %fusion.10), channel_id=1, replica_groups=mesh['row'=16,'col'=32] {'row','col'}, use_global_device_ids=true, to_apply=%region_10.11 | all-reduce | flops 128 | bytes 1024 | tf_op jit(solution)/shard_map/psum | solution.py:84
  486.8 0.5 fusion.14
  487.4 95.3 %psum.46 = f32[128]{0:T(128)S(1)} all-reduce(f32[128]{0:T(128)S(1)} %get-tuple-element.58), channel_id=1, replica_groups=mesh['row'=16,'col'=32] {'row','col'}, use_global_device_ids=true, to_apply=%region_12.13 | all-reduce | flops 128 | bytes 1024 | tf_op jit(solution)/shard_map/psum | solution.py:73
  582.7 2.6 collective-permute-start.15
  585.3 3.5 collective-permute-start.14
  589.6 1.2 collective-permute-done.14
  590.8 1.3 collective-permute-start.16
  592.1 4.0 collective-permute-start.17
  596.2 1.0 collective-permute-done.17
  597.8 102.0 %psum.47 = f32[128]{0:T(128)S(1)} all-reduce(f32[128]{0:T(128)S(1)} %fusion.12), channel_id=1, replica_groups=mesh['row'=16,'col'=32] {'row','col'}, use_global_device_ids=true, to_apply=%region_14.15 | all-reduce | flops 128 | bytes 1024 | tf_op jit(solution)/shard_map/psum | solution.py:84
  699.9 0.8 copy.172
  (128 shorter events, 8.3 us)
Async XLA Ops:
  6.5 15.1 %copy-start.1 = (f32[1,2,128,128]{3,2,1,0:T(8,128)S(1)}, f32[1,2,128,128]{3,2,1,0:T(8,128)}, u32[]{:S(2)}) copy-start(f32[1,2,128,128]{3,2,1,0:T(8,128)} %param.15) | copy-start | bytes 393220
  6.5 11.8 %copy-start.4 = (f32[1,2,2,32]{3,2,1,0:T(2,128)S(1)}, f32[1,2,2,32]{3,2,1,0:T(2,128)}, u32[]{:S(2)}) copy-start(f32[1,2,2,32]{3,2,1,0:T(2,128)} %param.19) | copy-start | bytes 1540
  6.5 95.8 %all-gather.2.cloned.1.call-start = ((), (), s32[]{:S(2)}) async-start(), calls=%async_computation | async-start | bytes 1081344 | tf_op jit(solution)/shard_map/all_gather | solution.py:148
  7.6 21.3 %collective-permute-start.2 = (f32[1,2,32,128]{2,3,1,0:T(8,128)S(1)}, f32[1,2,32,128]{2,3,1,0:T(8,128)S(1)}, u32[]{:S(2)}, u32[]{:S(2)}) collective-permute-start(f32[1,2,32,128]{2,3,1,0:T(8,128)S(1)} %bitcast.150), channel_id=1, source_target_pairs={{32,0},{64,32},{96,64},{128,96},{160,128},{192,160},{224,192},{256... | collective-permute-start | bytes 98312 | tf_op jit(solution)/shard_map/ppermute | solution.py:18
  16.4 12.6 %collective-permute-start.1 = (f32[1,2,32,128]{2,3,1,0:T(8,128)S(1)}, f32[1,2,32,128]{2,3,1,0:T(8,128)S(1)}, u32[]{:S(2)}, u32[]{:S(2)}) collective-permute-start(f32[1,2,32,128]{2,3,1,0:T(8,128)S(1)} %bitcast.151), channel_id=1, source_target_pairs={{0,32},{32,64},{64,96},{96,128},{128,160},{160,192},{192,224},{224... | collective-permute-start | bytes 98312 | tf_op jit(solution)/shard_map/ppermute | solution.py:15
  18.4 10.5 %collective-permute-start = (f32[1,1,32]{2,1,0:T(1,128)S(1)}, f32[1,1,32]{2,1,0:T(1,128)S(1)}, u32[]{:S(2)}, u32[]{:S(2)}) collective-permute-start(f32[1,1,32]{2,1,0:T(1,128)S(1)} %slice_bitcast_fusion.1), channel_id=1, source_target_pairs={{0,1},{1,2},{2,3},{3,4},{4,5},{5,6},{6,7},{7,8},{8,9},{9,10},{10,1... | collective-permute-start | bytes 392 | tf_op jit(solution)/shard_map/ppermute | solution.py:26
  19.7 1.9 copy-start.10
  19.7 16.1 %collective-permute-start.5 = (f32[1,2,32]{2,1,0:T(2,128)S(1)}, f32[1,2,32]{2,1,0:T(2,128)S(1)}, u32[]{:S(2)}, u32[]{:S(2)}) collective-permute-start(f32[1,2,32]{2,1,0:T(2,128)S(1)} %bitcast.184), channel_id=1, source_target_pairs={{0,32},{32,64},{64,96},{96,128},{128,160},{160,192},{192,224},{224... | collective-permute-start | bytes 776 | tf_op jit(solution)/shard_map/ppermute | solution.py:26
  23.2 0.7 copy-start.5
  23.8 2.7 copy-start
  24.1 0.7 copy-start.9
  24.8 0.7 copy-start.6
  24.8 0.7 copy-start.7
  25.6 0.7 copy-start.8
  26.5 0.7 copy-start.3
  27.9 0.9 copy-start.2
  29.1 5.3 collective-permute-start.3
  30.4 5.2 collective-permute-start.4
  151.0 10.8 %collective-permute-start.7 = (f32[1,2,32,128]{2,3,1,0:T(8,128)S(1)}, f32[1,2,32,128]{2,3,1,0:T(8,128)S(1)}, u32[]{:S(2)}, u32[]{:S(2)}) collective-permute-start(f32[1,2,32,128]{2,3,1,0:T(8,128)S(1)} %bitcast.142), channel_id=1, source_target_pairs={{32,0},{64,32},{96,64},{128,96},{160,128},{192,160},{224,192},{256... | collective-permute-start | bytes 98312 | tf_op jit(solution)/shard_map/ppermute | solution.py:18
  157.9 5.1 collective-permute-start.6
  163.1 5.4 collective-permute-start.8
  164.4 5.2 collective-permute-start.9
  370.0 6.6 collective-permute-start.11
  372.6 5.2 collective-permute-start.10
  377.9 5.4 collective-permute-start.12
  379.2 5.2 collective-permute-start.13
  582.7 6.8 collective-permute-start.15
  585.3 5.4 collective-permute-start.14
  590.8 5.4 collective-permute-start.16
  592.1 5.2 collective-permute-start.17
Sparse Core Ops, SparseCore 0:
  23.1 79.1 all-gather.1
where the time goes:
time: 709 us; the launch traced here: 707 us
  blocking collectives  498 us (70%)
  waiting for transfers between devices  75.2 us (11%)
  starting transfers between devices  57 us (8%)
  other arithmetic  49.2 us (7%)
  between operations  14.1 us (2%)
  local copies, waits for them, and re-layouts  9.8 us (1%)
    psum x3, blocking collectives, residual_product(): return lax.psum(inner_sum(residual, precond), ('row', 'col'))  295 us
    psum x2, blocking collectives, solve_separate(): curvature = lax.psum(inner_sum(direction, applied), ('row', 'col'))  204 us
    all_gather x1, waiting for transfers between devices, local(): gathered = lax.all_gather(drivers, 'col', axis=0, tiled=True)  66.4 us
    ppermute x8, starting transfers between devices, padded_2(): lax.ppermute(lax.slice_in_dim(block, block.shape[dim] - width, None, axis...  27.8 us
    ppermute x8, starting transfers between devices, padded_2(): lax.ppermute(lax.slice_in_dim(block, 0, width, axis=dim), axis, backward)  26 us
    another operation x4, other arithmetic, tile_inverse(): factors = jnp.linalg.cholesky(flat_blocks)  23.6 us
    another operation x3, other arithmetic, tile_inverse(): jax.scipy.linalg.cho_solve((factor, True), identity)  19.8 us
  transfers between devices with their start and end apart: 19, of which 11 were waited for; matrix products, arithmetic and copies ran while one was open for 1% of the time, Pallas kernels for 0%

commit v1 on v0

--- a/solution.py
+++ b/solution.py
@@ -145,7 +145,9 @@
     wanted = sink_net.reshape((sink_net.shape[2], sink_net.shape[3]))
     voltage = initial_voltage
     drivers = driver_voltage(voltage, driver_tile)
-    gathered = lax.all_gather(drivers, "col", axis=0, tiled=True)
+    gathered = jnp.concatenate(
+        lax.all_to_all(jnp.stack([drivers] * lax.axis_size("col")), "col", 0, 0), axis=0
+    )
     offsets = jnp.arange(col_count, dtype=jnp.int32)[:, None] * net_count
     values = jnp.take(gathered, (wanted + offsets).reshape(-1), axis=0).reshape(
         wanted.shape + (pattern_count,)

time: 709 us -> 655 us (0.924)
  waiting for transfers between devices: 75.2 us -> 29.7 us
  between operations: 14.1 us -> 0.77 us
    all_gather x1 -> x0, waiting for transfers between devices: 66.4 us -> none  [local(): gathered = lax.all_gather(drivers, 'col', axis=0, tiled=True)]
    all_to_all x0 -> x1, waiting for transfers between devices: none -> 13.5 us  [local(): lax.all_to_all(jnp.stack([drivers] * lax.axis_size('col')), 'col', 0, 0)]
    ppermute x8, waiting for transfers between devices: 1.06 us -> 11.5 us  [padded_2(): lax.ppermute(lax.slice_in_dim(block, 0, width, axis=dim), axis, backward)]
    ppermute x8, starting transfers between devices: 26 us -> 15.6 us  [padded_2(): lax.ppermute(lax.slice_in_dim(block, 0, width, axis=dim), axis, backward)]
    all_to_all x0 -> x1, starting transfers between devices: none -> 9.38 us  [local(): lax.all_to_all(jnp.stack([drivers] * lax.axis_size('col')), 'col', 0, 0)]
  transfers between devices with their start and end apart: 19 -> 19, of which waited for: 11 -> 9; matrix products, arithmetic and copies ran while one was open for 1% -> 1% of each run, Pallas kernels for 0% -> 0%
where the time goes in v1:
time: 655 us; the launch traced here: 654 us
  blocking collectives  497 us (76%)
  starting transfers between devices  63.5 us (10%)
  other arithmetic  47.6 us (7%)
  waiting for transfers between devices  29.7 us (5%)
  local copies, waits for them, and re-layouts  11 us (2%)
    psum x3, blocking collectives, residual_product(): return lax.psum(inner_sum(residual, precond), ('row', 'col'))  296 us
    psum x2, blocking collectives, solve_separate(): curvature = lax.psum(inner_sum(direction, applied), ('row', 'col'))  202 us
    ppermute x8, starting transfers between devices, padded_2(): lax.ppermute(lax.slice_in_dim(block, block.shape[dim] - width, None, axis...  34.2 us
    another operation x4, other arithmetic, tile_inverse(): factors = jnp.linalg.cholesky(flat_blocks)  23.6 us
    another operation x3, other arithmetic, tile_inverse(): jax.scipy.linalg.cho_solve((factor, True), identity)  19.8 us
    ppermute x8, starting transfers between devices, padded_2(): lax.ppermute(lax.slice_in_dim(block, 0, width, axis=dim), axis, backward)  15.6 us
    all_to_all x1, waiting for transfers between devices, local(): lax.all_to_all(jnp.stack([drivers] * lax.axis_size('col')), 'col', 0, 0)  13.5 us
  transfers between devices with their start and end apart: 19, of which 9 were waited for; matrix products, arithmetic and copies ran while one was open for 1% of the time, Pallas kernels for 0%

profile of v1, /device:TPU:1, one launch (start us, length us, event | category | flops | bytes accessed | tf_op | source)
XLA Modules:
  0.0 653.6 jit_solution(14563105003955530149)
XLA Ops:
  0.0 1.1 copy.150
  1.1 5.4 collective-permute-start.1
  6.5 4.7 collective-permute-start.2
  11.2 1.3 collective-permute-start
  12.5 3.0 collective-permute-start.5
  15.6 0.6 gather_fusion
  16.2 1.1 stack.2
  17.3 9.4 %all-to-all-start = ((f32[32,64,128]{2,1,0:T(8,128)}), f32[32,64,128]{2,1,0:T(8,128)S(1)}, u32[]{:S(2)}, u32[]{:S(2)}) async-start(f32[32,64,128]{2,1,0:T(8,128)} %stack.2), calls=%async_computation | async-start | bytes 2097152 | tf_op jit(solution)/shard_map/all_to_all | solution.py:149
  27.0 0.6 copy-done.5
  27.9 0.7 copy-done.6
  28.7 0.6 copy-done.9
  29.5 0.5 copy-done.7
  30.3 0.7 copy-done.3
  31.8 0.8 copy-done.2
  33.0 1.3 collective-permute-start.3
  34.3 4.0 collective-permute-start.4
  38.4 1.7 collective-permute-done.4
  40.4 13.5 %all-to-all-done = f32[32,64,128]{2,1,0:T(8,128)S(1)} async-done(((f32[32,64,128]{2,1,0:T(8,128)}), f32[32,64,128]{2,1,0:T(8,128)S(1)}, u32[]{:S(2)}, u32[]{:S(2)}) %all-to-all-start) | async-done | bytes 1048608 | tf_op jit(solution)/shard_map/all_to_all | solution.py:149
  54.0 2.4 scatter_custom_fusion
  56.7 23.5 %custom-call.11 = f32[2,128,128]{2,1,0:T(8,128)S(1)} custom-call(f32[2,128,128]{2,1,0:T(8,128)S(1)} %fusion.13), custom_call_target="Cholesky" | custom-call | tf_op jit(solution)/shard_map/jit(cholesky)/cholesky | solution.py:34
  80.4 19.7 %custom-call.12 = f32[2,1,128,128]{2,3,1,0:T(8,128)S(1)} custom-call(f32[2,1,128,128]{3,2,1,0:T(8,128)S(1)} %select_bitcast_fusion), custom_call_target="InvertDiagBlocksLowerTriangular" | custom-call | tf_op jit(solution)/shard_map/vmap(jit(_cho_solve))/triangular_solve | solution.py:35
  101.3 4.1 collective-permute-start.6
  105.4 1.9 collective-permute-start.7
  108.0 3.7 collective-permute-done.7
  111.8 1.3 collective-permute-start.8
  113.1 4.2 collective-permute-start.9
  117.4 0.9 collective-permute-done.9
  118.7 105.2 %all-reduce.1 = (f32[128]{0:T(128)S(1)}, f32[128]{0:T(128)S(1)}) all-reduce(f32[128]{0:T(128)S(1)} %multiply_reduce_fusion, f32[128]{0:T(128)S(1)} %fusion.8), channel_id=1, replica_groups=mesh['row'=16,'col'=32] {'row','col'}, use_global_device_ids=true, to_apply=%region_4.5 | all-reduce | flops 256 | bytes 2048 | tf_op jit(solution)/shard_map/psum | solution.py:73
  224.0 0.5 fusion.17
  224.5 95.4 %psum.44 = f32[128]{0:T(128)S(1)} all-reduce(f32[128]{0:T(128)S(1)} %get-tuple-element.56), channel_id=1, replica_groups=mesh['row'=16,'col'=32] {'row','col'}, use_global_device_ids=true, to_apply=%region_8.9 | all-reduce | flops 128 | bytes 1024 | tf_op jit(solution)/shard_map/psum | solution.py:73
  320.0 4.2 collective-permute-start.10
  324.2 1.9 collective-permute-start.11
  326.7 3.8 collective-permute-done.11
  330.6 1.3 collective-permute-start.12
  331.9 4.0 collective-permute-start.13
  336.0 1.0 collective-permute-done.13
  337.5 100.8 %psum.45 = f32[128]{0:T(128)S(1)} all-reduce(f32[128]{0:T(128)S(1)} %fusion.10), channel_id=1, replica_groups=mesh['row'=16,'col'=32] {'row','col'}, use_global_device_ids=true, to_apply=%region_10.11 | all-reduce | flops 128 | bytes 1024 | tf_op jit(solution)/shard_map/psum | solution.py:84
  438.3 0.5 fusion.14
  438.8 95.3 %psum.46 = f32[128]{0:T(128)S(1)} all-reduce(f32[128]{0:T(128)S(1)} %get-tuple-element.58), channel_id=1, replica_groups=mesh['row'=16,'col'=32] {'row','col'}, use_global_device_ids=true, to_apply=%region_12.13 | all-reduce | flops 128 | bytes 1024 | tf_op jit(solution)/shard_map/psum | solution.py:73
  534.2 4.4 collective-permute-start.14
  538.6 1.9 collective-permute-start.15
  540.5 0.4 fusion.5
  541.1 3.8 collective-permute-done.15
  545.0 1.3 collective-permute-start.16
  546.3 4.0 collective-permute-start.17
  550.4 1.0 collective-permute-done.17
  551.9 100.8 %psum.47 = f32[128]{0:T(128)S(1)} all-reduce(f32[128]{0:T(128)S(1)} %fusion.12), channel_id=1, replica_groups=mesh['row'=16,'col'=32] {'row','col'}, use_global_device_ids=true, to_apply=%region_14.15 | all-reduce | flops 128 | bytes 1024 | tf_op jit(solution)/shard_map/psum | solution.py:84
  652.8 0.8 copy.172
  (128 shorter events, 8.1 us)
Async XLA Ops:
  0.0 15.6 %copy-start.1 = (f32[1,2,128,128]{3,2,1,0:T(8,128)S(1)}, f32[1,2,128,128]{3,2,1,0:T(8,128)}, u32[]{:S(2)}) copy-start(f32[1,2,128,128]{3,2,1,0:T(8,128)} %param.15) | copy-start | bytes 393220
  0.0 11.2 %copy-start.4 = (f32[1,2,2,32]{3,2,1,0:T(2,128)S(1)}, f32[1,2,2,32]{3,2,1,0:T(2,128)}, u32[]{:S(2)}) copy-start(f32[1,2,2,32]{3,2,1,0:T(2,128)} %param.19) | copy-start | bytes 1540
  1.1 31.7 %collective-permute-start.1 = (f32[1,2,32,128]{2,3,1,0:T(8,128)S(1)}, f32[1,2,32,128]{2,3,1,0:T(8,128)S(1)}, u32[]{:S(2)}, u32[]{:S(2)}) collective-permute-start(f32[1,2,32,128]{2,3,1,0:T(8,128)S(1)} %bitcast.151), channel_id=1, source_target_pairs={{0,32},{32,64},{64,96},{96,128},{128,160},{160,192},{192,224},{224... | collective-permute-start | bytes 98312 | tf_op jit(solution)/shard_map/ppermute | solution.py:15
  6.5 26.4 %collective-permute-start.2 = (f32[1,2,32,128]{2,3,1,0:T(8,128)S(1)}, f32[1,2,32,128]{2,3,1,0:T(8,128)S(1)}, u32[]{:S(2)}, u32[]{:S(2)}) collective-permute-start(f32[1,2,32,128]{2,3,1,0:T(8,128)S(1)} %bitcast.152), channel_id=1, source_target_pairs={{32,0},{64,32},{96,64},{128,96},{160,128},{192,160},{224,192},{256... | collective-permute-start | bytes 98312 | tf_op jit(solution)/shard_map/ppermute | solution.py:18
  11.2 21.5 %collective-permute-start = (f32[1,1,32]{2,1,0:T(1,128)S(1)}, f32[1,1,32]{2,1,0:T(1,128)S(1)}, u32[]{:S(2)}, u32[]{:S(2)}) collective-permute-start(f32[1,1,32]{2,1,0:T(1,128)S(1)} %slice_bitcast_fusion.1), channel_id=1, source_target_pairs={{0,1},{1,2},{2,3},{3,4},{4,5},{5,6},{6,7},{7,8},{8,9},{9,10},{10,1... | collective-permute-start | bytes 392 | tf_op jit(solution)/shard_map/ppermute | solution.py:26
  12.5 3.0 copy-start.10
  12.5 27.8 %collective-permute-start.5 = (f32[1,2,32]{2,1,0:T(2,128)S(1)}, f32[1,2,32]{2,1,0:T(2,128)S(1)}, u32[]{:S(2)}, u32[]{:S(2)}) collective-permute-start(f32[1,2,32]{2,1,0:T(2,128)S(1)} %bitcast.186), channel_id=1, source_target_pairs={{0,32},{32,64},{64,96},{96,128},{128,160},{160,192},{192,224},{224... | collective-permute-start | bytes 776 | tf_op jit(solution)/shard_map/ppermute | solution.py:26
  17.3 36.6 %all-to-all-start = ((f32[32,64,128]{2,1,0:T(8,128)}), f32[32,64,128]{2,1,0:T(8,128)S(1)}, u32[]{:S(2)}, u32[]{:S(2)}) async-start(f32[32,64,128]{2,1,0:T(8,128)} %stack.2), calls=%async_computation | async-start | bytes 2097152 | tf_op jit(solution)/shard_map/all_to_all | solution.py:149
  26.9 0.7 copy-start.5
  27.6 2.8 copy-start
  27.9 0.7 copy-start.6
  28.7 0.7 copy-start.9
  29.4 0.7 copy-start.7
  29.4 0.7 copy-start.8
  30.3 0.7 copy-start.3
  31.7 0.9 copy-start.2
  33.0 5.5 collective-permute-start.3
  34.3 5.9 collective-permute-start.4
  101.3 6.6 %collective-permute-start.6 = (f32[1,2,32,128]{2,3,1,0:T(8,128)S(1)}, f32[1,2,32,128]{2,3,1,0:T(8,128)S(1)}, u32[]{:S(2)}, u32[]{:S(2)}) collective-permute-start(f32[1,2,32,128]{2,3,1,0:T(8,128)S(1)} %bitcast.143), channel_id=1, source_target_pairs={{0,32},{32,64},{64,96},{96,128},{128,160},{160,192},{192,224},{224... | collective-permute-start | bytes 98312 | tf_op jit(solution)/shard_map/ppermute | solution.py:15
  105.4 6.3 collective-permute-start.7
  111.8 5.6 collective-permute-start.8
  113.1 5.2 collective-permute-start.9
  320.0 6.6 %collective-permute-start.10 = (f32[1,2,32,128]{2,3,1,0:T(8,128)S(1)}, f32[1,2,32,128]{2,3,1,0:T(8,128)S(1)}, u32[]{:S(2)}, u32[]{:S(2)}) collective-permute-start(f32[1,2,32,128]{2,3,1,0:T(8,128)S(1)} %bitcast.147), channel_id=1, source_target_pairs={{0,32},{32,64},{64,96},{96,128},{128,160},{160,192},{192,224},{224... | collective-permute-start | bytes 98312 | tf_op jit(solution)/shard_map/ppermute | solution.py:15
  324.2 6.3 collective-permute-start.11
  330.6 5.4 collective-permute-start.12
  331.9 5.2 collective-permute-start.13
  534.2 6.8 %collective-permute-start.14 = (f32[1,2,32,128]{2,3,1,0:T(8,128)S(1)}, f32[1,2,32,128]{2,3,1,0:T(8,128)S(1)}, u32[]{:S(2)}, u32[]{:S(2)}) collective-permute-start(f32[1,2,32,128]{2,3,1,0:T(8,128)S(1)} %bitcast.154), channel_id=1, source_target_pairs={{0,32},{32,64},{64,96},{96,128},{128,160},{160,192},{192,224},{224... | collective-permute-start | bytes 98312 | tf_op jit(solution)/shard_map/ppermute | solution.py:15
  538.6 6.3 collective-permute-start.15
  545.0 5.4 collective-permute-start.16
  546.3 5.2 collective-permute-start.17
